TPU v7x, 512 devices: a whole 4x4x16 slice. The times are simulated.
512 devices in a mesh: col: 64 (over z, y), row: 8 (over x, core).
Axes of the slice: x: 4, y: 4, z: 16, core: 2. Of those that a mesh axis runs over, the one named last changes fastest.
Arguments:
- static_flex: float32 [8192, 32768], P('row', 'col'), may hold values from -6 to 6
- phi_slab: float32 [8192, 1024], P('row', 'col'), may hold values from -6 to 6
- phi_cols: float32 [32768, 1024], P('col', 'row'), may hold values from -6 to 6
- eigenvalues: float32 [1024], P('col'), may hold values from 8 to 128
Outputs:
- residual_flex: float32 [8192, 32768], P('row', 'col')
All inputs are finite; a program needn't handle non-finite values.
Results may differ from a plain program's by a relative error of at most 0.00005.
Values sent between devices are 32-bit elements; how exact they have to be, the bound alone decides.
A program may use at most 64 MiB of HBM per device.

v0:
```python
import jax
import jax.numpy as jnp
from jax import lax
from jax.sharding import Mesh
from jax.sharding import PartitionSpec as P

COL = ("col_0", "col_1")


def whole_of(value, axes, dim):
    result = value
    for number in range(len(axes) - 1, -1, -1):
        result = lax.all_gather(result, axes[number], axis=dim, tiled=True)
    return result


def from_everyone(value, axis):
    copies = jnp.broadcast_to(value, (lax.axis_size(axis), *value.shape))
    return lax.all_to_all(copies, axis, split_axis=0, concat_axis=0, tiled=True)


def joined_along(parts, dim):
    parts = jnp.moveaxis(parts, 0, dim)
    lengths = parts.shape
    return parts.reshape(*lengths[:dim], lengths[dim] * lengths[dim + 1], *lengths[dim + 2 :])


def gather_directly(value, axis, dim):
    parts = from_everyone(value, axis)
    return joined_along(parts, dim)


def outer_modes(left, right):
    return lax.dot_general(
        left,
        right,
        (((1,), (1,)), ((), ())),
        precision=lax.Precision.HIGHEST,
        preferred_element_type=jnp.float32,
    )


def local(static_flex, phi_slab, phi_cols, eigenvalues):
    scaled = phi_slab / eigenvalues[None, :]
    rows_all = whole_of(scaled, COL, 1)
    cols_all = gather_directly(phi_cols, "row", 1)
    result = static_flex - outer_modes(rows_all, cols_all)
    return result


def solution(mesh):
    torus = Mesh(mesh.devices.reshape(16, 4, mesh.shape["row"]), ("col_0", "col_1", "row"))
    placed = (P("row", COL), P("row", COL), P(COL, "row"), P(COL))
    return jax.shard_map(
        local, mesh=torus, in_specs=placed, out_specs=P("row", COL), check_vma=False
    )
```

profile of v0, /device:TPU:10, one launch (start us, length us, event | category | flops | bytes accessed | tf_op | source)
XLA Modules:
  0.0 119.6 jit_solution(15948946820837420017)
XLA Ops:
  6.5 0.0 all-gather.2.cloned.1.call-start
  6.5 0.9 broadcast_divide_fusion
  7.5 13.4 %all_gather.6 = f32[1024,64]{0,1:T(8,128)} all-gather(f32[1024,16]{0,1:T(8,128)S(1)} %broadcast_divide_fusion), channel_id=1, replica_groups=mesh['col_0'=16,'col_1'=4,'row'=8] {'col_1'}, dimensions={1}, use_global_device_ids=true | all-gather | bytes 327680 | tf_op jit(solution)/shard_map/all_gather | solution.py:13
  20.8 0.0 all-gather.2.cloned.1.call-update
  20.9 1.1 copy.5
  21.9 0.3 broadcast_in_dim.4
  22.2 31.1 %all_to_all.5 = f32[8,512,128]{1,2,0:T(8,128)S(1)} all-to-all(f32[8,512,128]{1,2,0:T(8,128)S(1)} %broadcast_in_dim.4), channel_id=1, replica_groups=mesh['col_0'=16,'col_1'=4,'row'=8] {'row'}, dimensions={0} | all-to-all | bytes 4194304 | tf_op jit(solution)/shard_map/all_to_all | solution.py:19
  53.4 49.5 %all-gather.2.cloned.1.call-done = f32[1024,1024]{0,1:T(8,128)} async-done(((f32[1024,64]{0,1:T(8,128)}), f32[1024,1024]{0,1:T(8,128)}) %all-gather.2.cloned.1.call-update) | async-done | bytes 4194320 | tf_op jit(solution)/shard_map/all_gather | solution.py:13
  102.9 9.8 %convolution_subtract_fusion = f32[1024,512]{1,0:T(8,128)} fusion(f32[1024,512]{1,0:T(8,128)} %param.4, f32[1024,1024]{0,1:T(8,128)} %all-gather.2.cloned.1.call-done, f32[512,1024]{0,1:T(8,128)S(1)} %bitcast.5), kind=kOutput, calls=%fused_computation | convolution fusion | flops 6442975232 | bytes 10485760 | tf_op jit(solution)/shard_map/dot_general | solution.py:34
Async XLA Ops:
  6.5 96.3 %all-gather.2.cloned.1.call-start = ((), (), s32[]{:S(2)}) async-start(), calls=%async_computation.1 | async-start | bytes 4456448 | tf_op jit(solution)/shard_map/all_gather | solution.py:13
Sparse Core Ops, SparseCore 0:
  21.0 81.8 all-gather.1
where the time goes:
time: 120 us
  waiting for transfers between devices  49.5 us (41%)
  blocking collectives  44.5 us (37%)
  between operations  13.4 us (11%)
  matrix products  9.84 us (8%)
  local copies, waits for them, and re-layouts  1.33 us (1%)
    all_gather x1, waiting for transfers between devices, whole_of(): result = lax.all_gather(result, axes[number], axis=dim, tiled=True)  49.5 us
    all_to_all x1, blocking collectives, from_everyone(): return lax.all_to_all(copies, axis, split_axis=0, concat_axis=0, tiled=True)  31.1 us
    all_gather x1, blocking collectives, whole_of(): result = lax.all_gather(result, axes[number], axis=dim, tiled=True)  13.4 us
    dot_general x1, matrix products, outer_modes(): lax.dot_general(left, right, (((1,), (1,)), ((), ())), precision=lax.Prec...  9.84 us
  transfers between devices with their start and end apart: 1, of which 1 were waited for; matrix products, arithmetic and copies ran while one was open for 1% of the time, Pallas kernels for 0%

commit v1 on v0

v1 whole, which is shorter than its diff:
```python
import functools

import jax
import jax.numpy as jnp
from jax import lax
from jax.experimental import pallas as pl
from jax.experimental.pallas import tpu as pltpu
from jax.sharding import PartitionSpec as P

MESH = pl.DeviceIdType.MESH
NZ, NY, NX = 16, 4, 4
CUT = 384
TILE = 256


def plan_names():
    names = []
    for sign in (1, -1):
        for d in range(1, 9):
            names.append(("Qz", sign, d))
            for dy in range(NY):
                names.append(("Pz", sign, d, dy))
        names.append(("Py", sign))
        names.append(("Py2", sign))
        for e in range(-7, 9):
            names.append(("Qy", e, sign))
            names.append(("Qy2", e, sign))
        names.append(("Bx", sign))
        names.append(("Bx2", sign))
        names.append(("Bc", sign))
        names.append(("Bc2", sign))
    names.append(("Bc0",))
    return {name: number for number, name in enumerate(names)}


NAMES = plan_names()


def kernel(eig, slab, cols, out, raw, at, ball, bh, bl, send_sem, recv_sem, local_sem):
    col, row = lax.axis_index("col"), lax.axis_index("row")
    z, y = col // NY, col % NY
    x, core = row // 2, row % 2
    modes, lanes = slab.shape
    half = modes // 2
    n = cols.shape[0]

    def mod(value, size):
        return lax.rem(value + 2 * size, size)

    def at_z(step):
        return {"col": mod(z + step, NZ) * NY + y}

    def at_y(step):
        return {"col": z * NY + mod(y + step, NY)}

    def at_x(step):
        return {"row": mod(x + step, NX) * 2 + core}

    partner = {"row": x * 2 + (1 - core)}

    def copy(name, ref, device):
        number = NAMES[name]
        return pltpu.make_async_remote_copy(
            src_ref=ref,
            dst_ref=ref,
            send_sem=send_sem.at[number],
            recv_sem=recv_sem.at[number],
            device_id=device,
            device_id_type=MESH,
        )

    sent = []

    def send(name, ref, device):
        move = copy(name, ref, device)
        move.start()
        sent.append(move)

    def arrive(name, ref):
        copy(name, ref, partner).wait_recv()

    def part(e, dy, which, rows=None):
        lane = pl.ds(0, CUT) if which == "P" else pl.ds(CUT, lanes - CUT)
        sub = pl.ds(0, modes) if rows is None else pl.ds(rows * half, half)
        return at.at[mod(z - e, NZ), mod(y - dy, NY), sub, lane]

    def half_of(sign):
        return 0 if sign > 0 else 1

    def block(dx, c, rows=None):
        sub = pl.ds(0, n) if rows is None else pl.ds(rows * (n // 2), n // 2)
        return ball.at[mod(x - dx, NX) * 2 + c, sub, :]

    load_slab = pltpu.make_async_copy(slab, raw, local_sem.at[0])
    load_cols = pltpu.make_async_copy(cols, ball.at[row], local_sem.at[1])
    load_slab.start()
    load_cols.start()
    barrier = pltpu.get_barrier_semaphore()
    for device in (at_z(1), at_z(-1), at_y(1), at_y(-1), at_x(1), at_x(-1), partner):
        pl.semaphore_signal(barrier, inc=1, device_id=device, device_id_type=MESH)
    load_slab.wait()
    index = lax.broadcasted_iota(jnp.int32, (modes, 128), 0)
    scale = jnp.zeros((modes, 128), jnp.float32)
    for k in range(modes):
        scale = jnp.where(index == k, eig[k], scale)
    for lane in range(0, lanes, 128):
        at[z, y, :, pl.ds(lane, 128)] = raw[:, pl.ds(lane, 128)] / scale
    load_cols.wait()
    pl.semaphore_wait(barrier, 7)

    for sign in (1, -1):
        send(("Qz", sign, 1), part(0, 0, "Q"), at_z(sign))
        send(("Py", sign), part(0, 0, "P"), at_y(sign))
    for sign in (1, -1):
        send(("Bx", sign), block(0, core), at_x(sign))
        send(("Pz", sign, 1, 0), part(0, 0, "P"), at_z(sign))
        send(("Qy", 0, sign), part(0, 0, "Q"), at_y(sign))
    send(("Bc0",), block(0, core), partner)

    def q_z(s):
        for sign in (1, -1):
            if s < 8:
                arrive(("Qz", sign, s), part(sign * s, 0, "Q"))
                rows = None if s < 7 else half_of(sign)
                send(("Qz", sign, s + 1), part(sign * s, 0, "Q", rows), at_z(sign))
            else:
                arrive(("Qz", sign, s), part(8, 0, "Q", half_of(sign)))
        for e in (s, -s) if s < 8 else (8,):
            for sign in (1, -1):
                send(("Qy", e, sign), part(e, 0, "Q"), at_y(sign))

    def q_y(s):
        for e in (s, -s) if 0 < s < 8 else (s,):
            for sign in (1, -1):
                arrive(("Qy", e, sign), part(e, sign, "Q"))
                send(("Qy2", e, sign), part(e, sign, "Q", half_of(sign)), at_y(sign))

    def q_y2(s):
        for e in (s, -s) if 0 < s < 8 else (s,):
            for sign in (1, -1):
                arrive(("Qy2", e, sign), part(e, 2, "Q", half_of(sign)))

    def p_z(s):
        for dy in (0, 1, -1, 2):
            for sign in (1, -1):
                if s < 8:
                    arrive(("Pz", sign, s, dy % NY), part(sign * s, dy, "P"))
                    rows = None if s < 7 else half_of(sign)
                    send(("Pz", sign, s + 1, dy % NY), part(sign * s, dy, "P", rows), at_z(sign))
                else:
                    arrive(("Pz", sign, s, dy % NY), part(8, dy, "P", half_of(sign)))

    def p_y():
        for sign in (1, -1):
            arrive(("Py", sign), part(0, sign, "P"))
            send(("Py2", sign), part(0, sign, "P", half_of(sign)), at_y(sign))
        for sign in (1, -1):
            for way in (1, -1):
                send(("Pz", way, 1, sign % NY), part(0, sign, "P"), at_z(way))

    def p_y2():
        for sign in (1, -1):
            arrive(("Py2", sign), part(0, 2, "P", half_of(sign)))
        for way in (1, -1):
            send(("Pz", way, 1, 2), part(0, 2, "P"), at_z(way))

    def b_x():
        for sign in (1, -1):
            arrive(("Bx", sign), block(sign, core))
            send(("Bx2", sign), block(sign, core, half_of(sign)), at_x(sign))
            send(("Bc", sign), block(sign, core), partner)

    def b_x2():
        for sign in (1, -1):
            arrive(("Bx2", sign), block(2, core, half_of(sign)))
            send(("Bc2", sign), block(2, core, half_of(sign)), partner)

    def b_c():
        arrive(("Bc0",), block(0, 1 - core))
        for sign in (1, -1):
            arrive(("Bc", sign), block(sign, 1 - core))
            arrive(("Bc2", sign), block(2, 1 - core, half_of(sign)))

        @pl.loop(0, 8)
        def _(r):
            value = ball[r]
            high = value.astype(jnp.bfloat16)
            bh[r] = high
            bl[r] = (value - high.astype(jnp.float32)).astype(jnp.bfloat16)

    groups = modes * NY * 2
    pair = mod(z // 2, NZ // 2)

    def compute(offsets, first=False):
        picks = [mod(pair + offset, NZ // 2) for offset in offsets]

        @pl.loop(0, lanes // TILE)
        def _(tile):
            sub = pl.ds(pl.multiple_of(tile * TILE, TILE), TILE)
            left = []
            for pick in picks:
                left.append(at[pl.ds(pick * 2, 2), :, :, sub].reshape(groups, TILE).T)
            left = jnp.concatenate(left, axis=1) if len(left) > 1 else left[0]
            high = left.astype(jnp.bfloat16)
            low = (left - high.astype(jnp.float32)).astype(jnp.bfloat16)
            right_high = [bh[pick] for pick in picks]
            right_low = [bl[pick] for pick in picks]
            lhs = jnp.concatenate([high, high, low], axis=1)
            rhs = jnp.concatenate(right_high + right_low + right_high, axis=1)
            total = lax.dot_general(lhs, rhs, (((1,), (1,)), ((), ())), preferred_element_type=jnp.float32)
            if first:
                out[sub, :] = total
            else:
                out[sub, :] += total

    q_z(1)
    p_y()
    b_x()
    q_y(0)
    p_y2()
    q_z(2)
    p_z(1)
    q_y(1)
    b_x2()
    q_z(3)
    p_z(2)
    q_y(2)
    q_z(4)
    p_z(3)
    q_y(3)
    b_c()
    q_y2(0)
    q_y2(1)
    compute((0,), first=True)
    q_z(5)
    p_z(4)
    q_y(4)
    q_y2(2)
    q_y2(3)
    compute((-1, 1))
    q_z(6)
    p_z(5)
    q_y(5)
    q_z(7)
    p_z(6)
    q_y(6)
    q_y2(4)
    q_y2(5)
    compute((-2, 2))
    q_z(8)
    p_z(7)
    q_y(7)
    q_y2(6)
    q_y(8)
    q_y2(7)
    compute((-3, 3))
    p_z(8)
    q_y2(8)
    compute((4,))
    for move in sent:
        move.wait_send()


def local(static_flex, phi_slab, phi_cols, eigenvalues):
    modes, lanes = phi_slab.shape[1], phi_slab.shape[0]
    n, depth = phi_cols.shape
    count = len(NAMES)
    update = pl.pallas_call(
        kernel,
        out_shape=jax.ShapeDtypeStruct((lanes, n), jnp.float32),
        in_specs=[
            pl.BlockSpec(memory_space=pltpu.SMEM),
            pl.BlockSpec(memory_space=pl.ANY),
            pl.BlockSpec(memory_space=pl.ANY),
        ],
        out_specs=pl.BlockSpec(memory_space=pltpu.VMEM),
        scratch_shapes=[
            pltpu.VMEM((modes, lanes), jnp.float32),
            pltpu.VMEM((NZ, NY, modes, lanes), jnp.float32),
            pltpu.VMEM((8, n, depth), jnp.float32),
            pltpu.VMEM((8, n, depth), jnp.bfloat16),
            pltpu.VMEM((8, n, depth), jnp.bfloat16),
            pltpu.SemaphoreType.DMA((count,)),
            pltpu.SemaphoreType.DMA((count,)),
            pltpu.SemaphoreType.DMA((2,)),
        ],
        compiler_params=pltpu.CompilerParams(
            collective_id=0, has_side_effects=True, vmem_limit_bytes=32 * 2**20
        ),
        cost_estimate=pl.CostEstimate(flops=3 * 2**30, bytes_accessed=8 * 2**20, transcendentals=0),
        name="gather_update",
    )(eigenvalues, phi_slab.T, phi_cols)
    return static_flex - update


def solution(mesh):
    placed = (P("row", "col"), P("row", "col"), P("col", "row"), P("col"))
    return jax.shard_map(local, mesh=mesh, in_specs=placed, out_specs=P("row", "col"), check_vma=False)
```

time: 120 us -> 59 us (0.49)
  the two profiles are of different devices: /device:TPU:10 before, /device:TPU:2 now
where the time goes in v1:
time: 59 us; the launch traced here: 58.8 us
  Pallas kernels  54.5 us (92%)
  local copies, waits for them, and re-layouts  2.45 us (4%)
  other arithmetic  1.8 us (3%)
    pallas_call x1, Pallas kernels, local(): pl.pallas_call(kernel, out_shape=jax.ShapeDtypeStruct((lanes, n), jnp.flo...  54.5 us
    unnamed x8, local copies, waits for them, and re-layouts  2.45 us
    sub x1, other arithmetic, local(): return static_flex - update  1.8 us

profile of v1, /device:TPU:2, one launch (start us, length us, event | category | flops | bytes accessed | tf_op | source)
XLA Modules:
  0.0 58.8 jit_solution(4930185611280603635)
XLA Ops:
  0.0 0.0 copy-start
  0.0 0.9 %copy-done = f32[512,128]{1,0:T(8,128)S(1)} copy-done((f32[512,128]{1,0:T(8,128)S(1)}, f32[512,128]{1,0:T(8,128)}, u32[]{:S(2)}) %copy-start) | copy-done | bytes 262168
  1.0 0.0 copy-start.1
  1.0 0.8 %copy-done.1 = f32[1024,16]{0,1:T(8,128)S(1)} copy-done((f32[1024,16]{0,1:T(8,128)S(1)}, f32[1024,16]{0,1:T(8,128)}, u32[]{:S(2)}) %copy-start.1) | copy-done | bytes 65560
  1.8 0.0 copy-start.2
  1.8 0.7 %copy-done.2 = f32[16]{0:T(128)S(1)} copy-done((f32[16]{0:T(128)S(1)}, f32[16]{0:T(128)}, u32[]{:S(2)}) %copy-start.2) | copy-done | bytes 88
  2.4 0.0 copy-start.3
  2.4 54.5 %gather_update.1 = f32[1024,512]{1,0:T(8,128)S(1)} custom-call(f32[16]{0:T(128)S(1)} %copy-done.2, f32[16,1024]{1,0:T(8,128)S(1)} %bitcast.1, f32[512,128]{1,0:T(8,128)S(1)} %copy-done), custom_call_target="tpu_custom_call" | custom-call | flops 3221225472 | bytes 8388608 | tf_op jit(solution)/shard_map/gather_update/pallas_call | solution.py:268
  57.0 0.0 copy-done.3
  57.0 1.8 %sub.3 = f32[1024,512]{1,0:T(8,128)} subtract(f32[1024,512]{1,0:T(8,128)S(1)} %copy-done.3, f32[1024,512]{1,0:T(8,128)S(1)} %gather_update.1) | non-fusion elementwise | flops 524288 | bytes 6291456 | tf_op jit(solution)/shard_map/sub | solution.py:293
Async XLA Ops:
  0.0 0.9 %copy-start = (f32[512,128]{1,0:T(8,128)S(1)}, f32[512,128]{1,0:T(8,128)}, u32[]{:S(2)}) copy-start(f32[512,128]{1,0:T(8,128)} %cols.1) | copy-start | bytes 786436
  1.0 0.8 %copy-start.1 = (f32[1024,16]{0,1:T(8,128)S(1)}, f32[1024,16]{0,1:T(8,128)}, u32[]{:S(2)}) copy-start(f32[1024,16]{0,1:T(8,128)} %param.5) | copy-start | bytes 196612
  1.8 0.7 %copy-start.2 = (f32[16]{0:T(128)S(1)}, f32[16]{0:T(128)}, u32[]{:S(2)}) copy-start(f32[16]{0:T(128)} %eig.1) | copy-start | bytes 196
  2.4 54.5 %copy-start.3 = (f32[1024,512]{1,0:T(8,128)S(1)}, f32[1024,512]{1,0:T(8,128)}, u32[]{:S(2)}) copy-start(f32[1024,512]{1,0:T(8,128)} %param.4) | copy-start | bytes 6291460
